TPU v7x, 256 devices: a whole 4x4x8 slice. The times are simulated.
256 devices in a mesh: chan: 128 (over y, z, x), tm: 2 (over core).
Axes of the slice: x: 4, y: 4, z: 8, core: 2. Of those that a mesh axis runs over, the one named last changes fastest.
Arguments:
- traces: float32 [16384, 8192], P('chan', 'tm'), may hold values from -600 to 600
- channel_ok: int32 [16384], P('chan'), may hold values 0 or 1
- time_taps: float32 [33], replicated, may hold values from -4 to 4
- space_taps: float32 [5], replicated, may hold values from -4 to 4
- pair_blocks: int32 [2048, 2], P('chan'), may hold values from 0 to 127, as said below
- pair_count: int32 [128], P('chan'), may hold values from 4 to 16, as said below
Outputs:
- stacks: float32 [2048, 201, 128], P(('chan', 'tm'))
Inputs may be any that keep to these rules, and one draw needn't show every extreme that they name: `pair_blocks`: a != b, |a - b| <= 4, and both a and b lie within 4 of the owner's index p. Owner p uses its first pair_count[p] slots; the other slots' pairs are ignored. Some owner uses all 16 slots.
All inputs are finite; a program needn't handle non-finite values. No bound on the sum of `channel_ok` on one device may be relied on, other than what follows from the above.
Results may differ from a plain program's by a relative error of at most 0.0049.
Values may be sent and summed in bfloat16 or wider, within the bound.
A program may use at most 128 MiB of HBM per device.

v0:
```python
import math

import jax
import jax.numpy as jnp
from jax import lax
from jax.sharding import PartitionSpec as P

SEG = 256
MAXLAG = 100
TAPS = 33
STAPS = 5
CUT = 4
SLOTS = 16
NFFT = 510
LAGS = 201


def padded_2(cells, sides, width):
    for axis, dim in sides:
        count = lax.axis_size(axis)
        ends = count - 1
        head = lax.slice_in_dim(cells, 0, width, axis=dim)
        tail = lax.slice_in_dim(cells, cells.shape[dim] - width, cells.shape[dim], axis=dim)
        cells = jnp.concatenate(
            [
                lax.ppermute(tail, axis, [(i, (i + 1) % count) for i in range(ends)]),
                cells,
                lax.ppermute(head, axis, [((i + 1) % count, i) for i in range(ends)]),
            ],
            axis=dim,
        )
    return cells


def passed_along(block, axis, distance):
    devices = range(lax.axis_size(axis))
    route = [(i - distance, i) for i in devices if i - distance in devices]
    return lax.ppermute(block, axis, route)


def forward_table():
    sample_pos = lax.broadcasted_iota(jnp.int32, (SEG, SEG), 0)
    bin_pos = lax.broadcasted_iota(jnp.int32, (SEG, SEG), 1)
    phase_angle = (sample_pos * bin_pos % NFFT).astype(jnp.float32) * (2.0 * math.pi / NFFT)
    return jnp.concatenate([jnp.cos(phase_angle), -jnp.sin(phase_angle)], axis=1).astype(
        jnp.bfloat16
    )


def inverse_table():
    lag_values = lax.broadcasted_iota(jnp.int32, (LAGS, SEG), 0) - MAXLAG
    bin_pos = lax.broadcasted_iota(jnp.int32, (LAGS, SEG), 1)
    phase_angle = (lag_values * bin_pos % NFFT).astype(jnp.float32) * (2.0 * math.pi / NFFT)
    weight = jnp.where((bin_pos == 0) | (bin_pos == SEG - 1), 1.0, 2.0) / NFFT
    return jnp.concatenate([weight * jnp.cos(phase_angle), -weight * jnp.sin(phase_angle)], axis=1)


def transform(segment_rows, dft_table):
    flat_rows = segment_rows.reshape(-1, SEG)
    spectrum = jnp.dot(flat_rows, dft_table, preferred_element_type=jnp.float32)
    return spectrum.astype(jnp.bfloat16).reshape(segment_rows.shape[:-1] + (2 * SEG,))


def to_lags(spectra_rows, lag_table):
    slot_rows, chan_rows, width = spectra_rows.shape
    flat_rows = spectra_rows.reshape(slot_rows * chan_rows, width)
    lagged = jnp.dot(
        flat_rows,
        jnp.transpose(lag_table),
        precision=lax.Precision.HIGHEST,
        preferred_element_type=jnp.float32,
    )
    return jnp.transpose(lagged.reshape(slot_rows, chan_rows, lag_table.shape[0]), (0, 2, 1))


def local(traces, channel_ok, time_taps, space_taps, pair_blocks, pair_count):
    chan_width, samples = traces.shape
    local_segs = samples // SEG
    masked = traces * channel_ok.astype(jnp.float32)[:, None]
    half_taps = (TAPS - 1) // 2
    padded = padded_2(masked, (("tm", 1),), half_taps)
    time_filtered = time_taps[0] * padded[:, 0:samples]
    for tap_index in range(1, TAPS):
        time_filtered = (
            time_filtered + time_taps[tap_index] * padded[:, tap_index : tap_index + samples]
        )
    half_space = (STAPS - 1) // 2
    rim_rows = padded_2(time_filtered, (("chan", 0),), half_space)
    filtered = space_taps[0] * rim_rows[0:chan_width]
    for tap_index in range(1, STAPS):
        filtered = filtered + space_taps[tap_index] * rim_rows[tap_index : tap_index + chan_width]
    segment_view = filtered.reshape(chan_width, local_segs, SEG)
    seg_power = jnp.mean(segment_view * segment_view, axis=2, keepdims=True)
    whitened = (segment_view / jnp.sqrt(seg_power + 1e-05)).astype(jnp.bfloat16)
    dft_table = forward_table()
    own_spec = transform(whitened, dft_table)
    pieces = []
    for offset in range(-CUT, CUT + 1):
        if offset == 0:
            pieces.append(own_spec)
        else:
            pieces.append(passed_along(own_spec, "chan", -offset))
    window = jnp.stack(pieces)
    owner_index = lax.axis_index("chan")

    def correlate(pair_item):
        first_block, second, alive = pair_item
        left_spec = lax.dynamic_index_in_dim(
            window, first_block - owner_index + CUT, 0, keepdims=False
        ).astype(jnp.float32)
        right_spec = lax.dynamic_index_in_dim(
            window, second - owner_index + CUT, 0, keepdims=False
        ).astype(jnp.float32)
        left_re, left_im = (left_spec[..., :SEG], left_spec[..., SEG:])
        right_re, right_im = (right_spec[..., :SEG], right_spec[..., SEG:])
        cross_re = jnp.sum(left_re * right_re + left_im * right_im, axis=1)
        cross_im = jnp.sum(left_im * right_re - left_re * right_im, axis=1)
        return jnp.concatenate([cross_re, cross_im], axis=1) * alive

    slot_index = jnp.arange(SLOTS, dtype=jnp.int32)
    alive_flag = (slot_index < pair_count[0]).astype(jnp.float32)
    cross_spec = lax.map(correlate, (pair_blocks[:, 0], pair_blocks[:, 1], alive_flag))
    lag_table = inverse_table()
    stack_scale = 1.0 / math.sqrt(local_segs * lax.axis_size("tm") * SEG)
    lagged_all = to_lags(cross_spec, lag_table)
    lagged = lax.psum_scatter(lagged_all, "tm", scatter_dimension=0, tiled=True)
    return lagged * stack_scale


def solution(mesh):
    return jax.shard_map(
        local,
        mesh=mesh,
        in_specs=(P("chan", "tm"), P("chan"), P(), P(), P("chan", None), P("chan")),
        out_specs=P(("chan", "tm"), None, None),
        check_vma=False,
    )
```

profile of v0, /device:TPU:1, one launch (start us, length us, event | category | flops | bytes accessed | tf_op | source)
XLA Modules:
  0.0 589.0 jit_solution(11586331116654356773)
XLA Ops:
  10.5 5.1 collective-permute-start.1
  18.2 43.2 %fusion.12 = f32[128,4096]{1,0:T(8,128)S(1)} fusion(f32[128,16]{1,0:T(8,128)S(1)} %collective-permute-done.1, f32[128,16]{1,0:T(8,128)S(1)} %collective-permute-done, f32[128,4096]{1,0:T(8,128)S(1)} %broadcast_multiply_fusion, f32[]{:T(128)} %bitcast.43, f32[]{:T(128)} %bitcast.42, f32[]{:T(128)} %bitcast.41, f32[]{:T(128)} %bitcast.40, f32[]{:T(128)} %bitcast.39, ...), kind=kLoop, calls=%fused_computation.52 | loop fusion | flops 50855936 | bytes 4210820 | tf_op jit(solution)/shard_map/add | solution.py:85
  65.3 3.2 collective-permute-done.3
  68.5 4.6 fusion.126
  81.0 3.8 collective-permute-start.4
  84.9 8.0 %collective-permute-start.5 = (bf16[128,16,512]{2,1,0:T(8,128)(2,1)S(1)}, bf16[128,16,512]{2,1,0:T(8,128)(2,1)}, u32[]{:S(2)}, u32[]{:S(2)}) collective-permute-start(bf16[128,16,512]{2,1,0:T(8,128)(2,1)S(1)} %bitcast.100), channel_id=1, source_target_pairs={{0,6},{2,8},{4,10},{6,12},{8,14},{10,16},{12,18},{14,20},{16,22},{... | collective-permute-start | bytes 6291464 | tf_op jit(solution)/shard_map/ppermute | solution.py:38
  95.5 3.1 collective-permute-start.7
  100.6 28.6 %collective-permute-done.4 = bf16[128,16,512]{2,1,0:T(8,128)(2,1)S(1)} collective-permute-done((bf16[128,16,512]{2,1,0:T(8,128)(2,1)S(1)}, bf16[128,16,512]{2,1,0:T(8,128)(2,1)S(1)}, u32[]{:S(2)}, u32[]{:S(2)}) %collective-permute-start.4) | collective-permute-done | bytes 2097184 | tf_op jit(solution)/shard_map/ppermute | solution.py:38
  132.8 137.8 %collective-permute-done.5 = bf16[128,16,512]{2,1,0:T(8,128)(2,1)} collective-permute-done((bf16[128,16,512]{2,1,0:T(8,128)(2,1)S(1)}, bf16[128,16,512]{2,1,0:T(8,128)(2,1)}, u32[]{:S(2)}, u32[]{:S(2)}) %collective-permute-start.5) | collective-permute-done | bytes 2097184 | tf_op jit(solution)/shard_map/ppermute | solution.py:38
  280.6 8.6 %collective-permute-done.8 = bf16[128,16,512]{2,1,0:T(8,128)(2,1)} collective-permute-done((bf16[128,16,512]{2,1,0:T(8,128)(2,1)S(1)}, bf16[128,16,512]{2,1,0:T(8,128)(2,1)}, u32[]{:S(2)}, u32[]{:S(2)}) %collective-permute-start.8) | collective-permute-done | bytes 2097184 | tf_op jit(solution)/shard_map/ppermute | solution.py:38
  292.7 49.0 %collective-permute-done.10 = bf16[128,16,512]{2,1,0:T(8,128)(2,1)S(1)} collective-permute-done((bf16[128,16,512]{2,1,0:T(8,128)(2,1)S(1)}, bf16[128,16,512]{2,1,0:T(8,128)(2,1)S(1)}, u32[]{:S(2)}, u32[]{:S(2)}) %collective-permute-start.10) | collective-permute-done | bytes 2097184 | tf_op jit(solution)/shard_map/ppermute | solution.py:38
  341.9 21.3 %collective-permute-done.11 = bf16[128,16,512]{2,1,0:T(8,128)(2,1)S(1)} collective-permute-done((bf16[128,16,512]{2,1,0:T(8,128)(2,1)S(1)}, bf16[128,16,512]{2,1,0:T(8,128)(2,1)S(1)}, u32[]{:S(2)}, u32[]{:S(2)}) %collective-permute-start.11) | collective-permute-done | bytes 2097184 | tf_op jit(solution)/shard_map/ppermute | solution.py:38
  363.4 6.5 %copy-done = bf16[9,128,16,512]{3,2,1,0:T(8,128)(2,1)} copy-done((bf16[9,128,16,512]{3,2,1,0:T(8,128)(2,1)}, bf16[9,128,16,512]{3,2,1,0:T(8,128)(2,1)S(1)}, u32[]{:S(2)}) %copy-start) | copy-done | bytes 18874392
  369.9 142.9 %while.13 = (s32[]{:T(128)}, f32[16,128,512]{2,1,0:T(8,128)}, s32[16]{0:T(128)S(1)}, s32[]{:T(128)}, bf16[9,128,16,512]{3,2,1,0:T(8,128)(2,1)}, /*index=5*/s32[1...) while((s32[]{:T(128)}, f32[16,128,512]{2,1,0:T(8,128)}, ...), condition=%wide.region_4.5_spmd, body=%wide.region_1.4_spmd.sunk | while | flops 6357004 | bytes 21759244 | solution.py:122
  372.2 3.4 bitcast_convert_fusion.3
  381.1 3.4 bitcast_convert_fusion.3
  390.1 3.4 bitcast_convert_fusion.3
  399.0 3.4 bitcast_convert_fusion.3
  407.9 3.4 bitcast_convert_fusion.3
  416.9 3.4 bitcast_convert_fusion.3
  425.8 3.4 bitcast_convert_fusion.3
  434.7 3.4 bitcast_convert_fusion.3
  443.6 3.4 bitcast_convert_fusion.3
  452.6 3.4 bitcast_convert_fusion.3
  461.5 3.4 bitcast_convert_fusion.3
  470.5 3.4 bitcast_convert_fusion.3
  479.4 3.4 bitcast_convert_fusion.3
  488.3 3.4 bitcast_convert_fusion.3
  497.2 3.4 bitcast_convert_fusion.3
  506.2 3.4 bitcast_convert_fusion.3
  512.8 6.1 %fusion.106 = f32[16,128,201]{1,2,0:T(8,128)S(1)} fusion(f32[16,128,512]{2,1,0:T(8,128)} %get-tuple-element.114, f32[201,256]{1,0:T(8,128)S(1)} %get-tuple-element.140, f32[201,256]{1,0:T(8,128)S(1)} %get-tuple-element.139), kind=kOutput, calls=%fused_computation.186 | convolution fusion | flops 2529268224 | bytes 6252544 | tf_op jit(solution)/shard_map/dot_general | solution.py:67
  520.6 59.4 %reduce-scatter.2.cloned.1.call-done = f32[8,201,128]{2,0,1:T(8,128)} async-done(((f32[16,201,128]{2,0,1:T(8,128)}), f32[8,201,128]{2,0,1:T(8,128)}) %reduce-scatter.2.cloned.1.call-update) | async-done | bytes 823312 | tf_op jit(solution)/shard_map/reduce_scatter | solution.py:126
  (136 shorter events, 113.6 us)
Async XLA Ops:
  6.5 573.5 %reduce-scatter.2.cloned.1.call-start = ((), (), s32[]{:S(2)}) async-start(), calls=%async_computation.1 | async-start | bytes 2469888 | tf_op jit(solution)/shard_map/reduce_scatter | solution.py:126
  7.2 9.6 %copy-start.2 = (f32[33]{0:T(128)S(1)}, f32[33]{0:T(128)}, u32[]{:S(2)}) copy-start(f32[33]{0:T(128)} %param.10) | copy-start | bytes 400
  9.2 9.0 %collective-permute-start = (f32[128,16]{1,0:T(8,128)S(1)}, f32[128,16]{1,0:T(8,128)S(1)}, u32[]{:S(2)}, u32[]{:S(2)}) collective-permute-start(f32[128,16]{1,0:T(8,128)S(1)} %get-tuple-element.137), channel_id=1, source_target_pairs={{0,1},{2,3},{4,5},{6,7},{8,9},{10,11},{12,13},{14,15},{16,17},{18,... | collective-permute-start | bytes 24584 | tf_op jit(solution)/shard_map/ppermute | solution.py:26
  10.5 7.7 %collective-permute-start.1 = (f32[128,16]{1,0:T(8,128)S(1)}, f32[128,16]{1,0:T(8,128)S(1)}, u32[]{:S(2)}, u32[]{:S(2)}) collective-permute-start(f32[128,16]{1,0:T(8,128)S(1)} %get-tuple-element.138), channel_id=1, source_target_pairs={{1,0},{3,2},{5,4},{7,6},{9,8},{11,10},{13,12},{15,14},{17,16},{19,... | collective-permute-start | bytes 24584 | tf_op jit(solution)/shard_map/ppermute | solution.py:28
  18.2 46.4 %copy-start.3 = (f32[5]{0:T(128)S(1)}, f32[5]{0:T(128)}, u32[]{:S(2)}) copy-start(f32[5]{0:T(128)} %param.11) | copy-start | bytes 64
  61.5 3.8 collective-permute-start.2
  63.3 5.2 collective-permute-start.3
  78.7 21.9 %copy-start.4 = (s32[16,2]{0,1:T(2,128)S(1)}, s32[16,2]{0,1:T(2,128)}, u32[]{:S(2)}) copy-start(s32[16,2]{0,1:T(2,128)} %param.12) | copy-start | bytes 388
  81.0 48.2 %collective-permute-start.4 = (bf16[128,16,512]{2,1,0:T(8,128)(2,1)S(1)}, bf16[128,16,512]{2,1,0:T(8,128)(2,1)S(1)}, u32[]{:S(2)}, u32[]{:S(2)}) collective-permute-start(bf16[128,16,512]{2,1,0:T(8,128)(2,1)S(1)} %bitcast.99), channel_id=1, source_target_pairs={{0,8},{2,10},{4,12},{6,14},{8,16},{10,18},{12,20},{14,22},{16,24},... | collective-permute-start | bytes 6291464 | tf_op jit(solution)/shard_map/ppermute | solution.py:38
  84.9 185.7 %collective-permute-start.5 = (bf16[128,16,512]{2,1,0:T(8,128)(2,1)S(1)}, bf16[128,16,512]{2,1,0:T(8,128)(2,1)}, u32[]{:S(2)}, u32[]{:S(2)}) collective-permute-start(bf16[128,16,512]{2,1,0:T(8,128)(2,1)S(1)} %bitcast.100), channel_id=1, source_target_pairs={{0,6},{2,8},{4,10},{6,12},{8,14},{10,16},{12,18},{14,20},{16,22},{... | collective-permute-start | bytes 6291464 | tf_op jit(solution)/shard_map/ppermute | solution.py:38
  92.9 180.7 %collective-permute-start.6 = (bf16[128,16,512]{2,1,0:T(8,128)(2,1)S(1)}, bf16[128,16,512]{2,1,0:T(8,128)(2,1)}, u32[]{:S(2)}, u32[]{:S(2)}) collective-permute-start(bf16[128,16,512]{2,1,0:T(8,128)(2,1)S(1)} %bitcast.101), channel_id=1, source_target_pairs={{0,4},{2,6},{4,8},{6,10},{8,12},{10,14},{12,16},{14,18},{16,20},{1... | collective-permute-start | bytes 6291464 | tf_op jit(solution)/shard_map/ppermute | solution.py:38
  95.5 183.1 %collective-permute-start.7 = (bf16[128,16,512]{2,1,0:T(8,128)(2,1)S(1)}, bf16[128,16,512]{2,1,0:T(8,128)(2,1)}, u32[]{:S(2)}, u32[]{:S(2)}) collective-permute-start(bf16[128,16,512]{2,1,0:T(8,128)(2,1)S(1)} %bitcast.102), channel_id=1, source_target_pairs={{0,2},{2,4},{4,6},{6,8},{8,10},{10,12},{12,14},{14,16},{16,18},{18... | collective-permute-start | bytes 6291464 | tf_op jit(solution)/shard_map/ppermute | solution.py:38
  98.6 190.5 %collective-permute-start.8 = (bf16[128,16,512]{2,1,0:T(8,128)(2,1)S(1)}, bf16[128,16,512]{2,1,0:T(8,128)(2,1)}, u32[]{:S(2)}, u32[]{:S(2)}) collective-permute-start(bf16[128,16,512]{2,1,0:T(8,128)(2,1)S(1)} %bitcast.103), channel_id=1, source_target_pairs={{2,0},{4,2},{6,4},{8,6},{10,8},{12,10},{14,12},{16,14},{18,16},{20... | collective-permute-start | bytes 6291464 | tf_op jit(solution)/shard_map/ppermute | solution.py:38
  129.2 1.3 copy-start.1
  130.5 160.4 %collective-permute-start.9 = (bf16[128,16,512]{2,1,0:T(8,128)(2,1)S(1)}, bf16[128,16,512]{2,1,0:T(8,128)(2,1)}, u32[]{:S(2)}, u32[]{:S(2)}) collective-permute-start(bf16[128,16,512]{2,1,0:T(8,128)(2,1)S(1)} %bitcast.104), channel_id=1, source_target_pairs={{4,0},{6,2},{8,4},{10,6},{12,8},{14,10},{16,12},{18,14},{20,16},{2... | collective-permute-start | bytes 6291464 | tf_op jit(solution)/shard_map/ppermute | solution.py:38
  270.6 71.2 %collective-permute-start.10 = (bf16[128,16,512]{2,1,0:T(8,128)(2,1)S(1)}, bf16[128,16,512]{2,1,0:T(8,128)(2,1)S(1)}, u32[]{:S(2)}, u32[]{:S(2)}) collective-permute-start(bf16[128,16,512]{2,1,0:T(8,128)(2,1)S(1)} %bitcast.105), channel_id=1, source_target_pairs={{6,0},{8,2},{10,4},{12,6},{14,8},{16,10},{18,12},{20,14},{22,16},{... | collective-permute-start | bytes 6291464 | tf_op jit(solution)/shard_map/ppermute | solution.py:38
  273.6 89.6 %collective-permute-start.11 = (bf16[128,16,512]{2,1,0:T(8,128)(2,1)S(1)}, bf16[128,16,512]{2,1,0:T(8,128)(2,1)S(1)}, u32[]{:S(2)}, u32[]{:S(2)}) collective-permute-start(bf16[128,16,512]{2,1,0:T(8,128)(2,1)S(1)} %bitcast.106), channel_id=1, source_target_pairs={{8,0},{10,2},{12,4},{14,6},{16,8},{18,10},{20,12},{22,14},{24,16},... | collective-permute-start | bytes 6291464 | tf_op jit(solution)/shard_map/ppermute | solution.py:38
  363.4 6.5 %copy-start = (bf16[9,128,16,512]{3,2,1,0:T(8,128)(2,1)}, bf16[9,128,16,512]{3,2,1,0:T(8,128)(2,1)S(1)}, u32[]{:S(2)}) copy-start(bf16[9,128,16,512]{3,2,1,0:T(8,128)(2,1)S(1)} %bitcast_dynamic-update-slice_fusion) | copy-start | bytes 56623108
Sparse Core Ops, SparseCore 0:
  520.8 59.2 reduce-scatter.1
where the time goes:
time: 591 us; the launch traced here: 589 us
  waiting for transfers between devices  308 us (52%)
  other arithmetic  153 us (26%)
  local copies, waits for them, and re-layouts  54.1 us (9%)
  starting transfers between devices  32.4 us (5%)
  loops' own time  18.8 us (3%)
  between operations  14.3 us (2%)
  matrix products  8.49 us (1%)
    ppermute x8, waiting for transfers between devices, passed_along(): return lax.ppermute(block, axis, route)  245 us
    reduce_scatter x1, waiting for transfers between devices, local(): lagged = lax.psum_scatter(lagged_all, 'tm', scatter_dimension=0, tiled=True)  59.4 us
    convert_element_type x16, other arithmetic, correlate(): left_spec = lax.dynamic_index_in_dim(window, first_block - owner_index +...  53.9 us
    add x1, other arithmetic, local(): time_filtered + time_taps[tap_index] * padded[:, tap_index:tap_index + sa...  43.2 us
    dynamic_slice x48, local copies, waits for them, and re-layouts, local(): lax.map(correlate, (pair_blocks[:, 0], pair_blocks[:, 1], alive_flag))  27.8 us
    ppermute x8, starting transfers between devices, passed_along(): return lax.ppermute(block, axis, route)  22.9 us
    reduce_sum x16, other arithmetic, correlate(): cross_re = jnp.sum(left_re * right_re + left_im * right_im, axis=1)  21.7 us
    dynamic_update_slice x16, other arithmetic, local(): lax.map(correlate, (pair_blocks[:, 0], pair_blocks[:, 1], alive_flag))  20.7 us
  transfers between devices with their start and end apart: 13, of which 7 were waited for; matrix products, arithmetic and copies ran while one was open for 3% of the time, Pallas kernels for 0%

commit v1 on v0

v1 whole, which is shorter than its diff:
```python
import functools
import math

import jax
import jax.numpy as jnp
import ml_dtypes
import numpy as np
from jax import lax
from jax.experimental import pallas as pl
from jax.experimental.pallas import tpu as pltpu
from jax.sharding import PartitionSpec as P

SEG = 256
MAXLAG = 100
TAPS = 33
STAPS = 5
CUT = 4
SLOTS = 16
NFFT = 510
LAGS = 201
LAGROWS = 208
BLOCK = 128
GX = 4
CORES = 2
GROUPS = GX * CORES
QG = BLOCK // GROUPS
WIN = 8
PAD = 128
HALF = (TAPS - 1) // 2

BF16 = jnp.bfloat16
F32 = jnp.float32
MESH_ID = pl.DeviceIdType.MESH

OWN_PAIRS = (
    [(i, j) for i in (0, 1) for j in range(2, 6) if j - i <= CUT]
    + [(i, j) for i in range(2, 6) for j in range(i + 1, 6)]
    + [(i, j) for i in (2, 3) for j in (6, 7) if j - i <= CUT]
)
N_DOWN = 7
N_IN = 6
N_UP = 3
N_OWN = len(OWN_PAIRS)
FROM_DN = N_IN + N_UP
FROM_UP = N_DOWN + N_IN
N_ALL = FROM_DN + N_OWN + FROM_UP


def pair_positions():
    table = np.zeros((12 * CUT,), np.int32)
    rel = [(i + 2, j + 2) for i, j in OWN_PAIRS]
    entries = (
        [(i - GX, j - GX) for i, j in rel[N_DOWN:]]
        + rel
        + [(i + GX, j + GX) for i, j in rel[: N_DOWN + N_IN]]
    )
    for spot, (low, high) in enumerate(entries):
        table[low * CUT + high - low - 1] = spot
    return table


def split_np(table):
    high = table.astype(ml_dtypes.bfloat16)
    low = (table - high.astype(np.float64)).astype(ml_dtypes.bfloat16)
    return np.stack([high, low])


def forward_np():
    phase = (np.arange(SEG)[:, None] * np.arange(SEG)[None, :] % NFFT) * (2.0 * np.pi / NFFT)
    return np.concatenate([np.cos(phase), -np.sin(phase)], axis=1).astype(ml_dtypes.bfloat16)


def inverse_np(scale):
    lag = np.arange(LAGS)[None, :] - MAXLAG
    bins = np.arange(SEG)[:, None]
    phase = (lag * bins % NFFT) * (2.0 * np.pi / NFFT)
    weight = np.where((bins == 0) | (bins == SEG - 1), 1.0, 2.0) / NFFT * scale
    table = np.zeros((2 * SEG, SEG), np.float64)
    table[:SEG, :LAGS] = weight * np.cos(phase)
    table[SEG:, :LAGS] = -weight * np.sin(phase)
    return split_np(table)


def order_np():
    table = np.zeros((2, LAGROWS, SEG), ml_dtypes.bfloat16)
    for lag in range(LAGS):
        table[0, lag, lag] = 1.0
        table[1, lag, LAGS - 1 - lag] = 1.0
    return table


def halves(value):
    high = value.astype(BF16)
    return high, (value - high.astype(F32)).astype(BF16)


def dot(a, b):
    return jnp.dot(a, b, preferred_element_type=F32)


def kernel(
    n_chan,
    taps,
    staps,
    pairs,
    count,
    lut,
    ok_row,
    pairs_v,
    fwd,
    inv,
    order,
    traces,
    out,
    xp,
    xh,
    xl,
    band,
    edge,
    rim,
    tfb,
    w,
    r,
    xs,
    c,
    pt,
    f,
    g,
    pbv,
    pbs,
    tr_sem,
    halo_s,
    halo_r,
    pb_s,
    pb_r,
    pb_l,
    x_s,
    x_r,
    z_s,
    z_r,
    p_s,
    p_r,
    f_s,
    f_r,
):
    samples = traces.shape[1]
    n_seg = samples // SEG
    n_chunk = x_s.shape[0]
    per = n_seg // n_chunk
    lines = n_chan // GX
    me = lax.axis_index("chan")
    core = lax.axis_index("tm")
    line = me // GX
    pos = me % GX
    group = pos * CORES + core
    sibling = 1 - core
    nxt = (me + 1) % n_chan
    prv = (me + n_chan - 1) % n_chan
    up = ((line + 1) % lines) * GX + pos
    down = ((line + lines - 1) % lines) * GX + pos
    offsets = [(dx, dt) for dx in range(GX) for dt in range(CORES)]

    def peer(dx, dt):
        return (pos + dx) % GX, (core + dt) % CORES

    load = pltpu.make_async_copy(traces, xp.at[:, pl.ds(PAD, samples)], tr_sem)
    load.start()

    barrier = pltpu.get_barrier_semaphore()
    for dx, dt in offsets[1:]:
        px, pc = peer(dx, dt)
        pl.semaphore_signal(
            barrier, inc=1, device_id=(line * GX + px, pc), device_id_type=MESH_ID
        )
    for other in (up, down, nxt, prv):
        pl.semaphore_signal(barrier, inc=1, device_id=(other, core), device_id_type=MESH_ID)

    band[...] = jnp.zeros_like(band)
    row = lax.broadcasted_iota(jnp.int32, (PAD, PAD), 0)
    col = lax.broadcasted_iota(jnp.int32, (PAD, PAD), 1)
    for diff in range(3):
        index = row - col + (PAD * diff - (PAD - HALF))
        tile = jnp.zeros((PAD, PAD), F32)
        for tap in range(TAPS):
            tile = jnp.where(index == tap, taps[tap], tile)
        high, low = halves(tile)
        for cb in range(2):
            rb = cb + diff
            band[0, rb * PAD : (rb + 1) * PAD, cb * PAD : (cb + 1) * PAD] = high
            band[1, rb * PAD : (rb + 1) * PAD, cb * PAD : (cb + 1) * PAD] = low
    okb = jnp.broadcast_to(ok_row[...], (BLOCK, BLOCK)).astype(F32)
    ok_col = jnp.sum(jnp.where(row == col, okb, 0.0), axis=1, keepdims=True)
    zero_at = pl.multiple_of(core * 0 + jnp.where(core == 0, 0, PAD + samples), PAD)
    xp[:, pl.ds(zero_at, PAD)] = jnp.zeros((BLOCK, PAD), F32)

    load.wait()
    pl.semaphore_wait(barrier, len(offsets) - 1 + 4)

    src_at = pl.multiple_of(jnp.where(core == 0, samples, PAD), PAD)
    dst_at = pl.multiple_of(jnp.where(core == 0, 0, PAD + samples), PAD)
    halo = pltpu.make_async_remote_copy(
        xp.at[:, pl.ds(src_at, PAD)],
        xp.at[:, pl.ds(dst_at, PAD)],
        halo_s.at[0],
        halo_r.at[0],
        device_id=(me, sibling),
        device_id_type=MESH_ID,
    )
    halo.start()

    def pair_copy(dx):
        return pltpu.make_async_remote_copy(
            pairs_v,
            pbv.at[pos],
            pb_s.at[dx - 1],
            pb_r.at[dx - 1],
            device_id=(line * GX + (pos + dx) % GX, core),
            device_id_type=MESH_ID,
        )

    for dx in range(1, GX):
        pair_copy(dx).start()
    pbv[pos] = pairs_v[...]

    halo.wait()

    def mask_step(i, carry):
        at = pl.multiple_of(i * PAD, PAD)
        high, low = halves(xp[:, pl.ds(at, PAD)] * ok_col)
        xh[:, pl.ds(at, PAD)] = high
        xl[:, pl.ds(at, PAD)] = low
        return carry

    lax.fori_loop(0, samples // PAD + 2, mask_step, 0)

    def time_filter(windows_h, windows_l):
        high = jnp.concatenate(windows_h, axis=0)
        low = jnp.concatenate(windows_l, axis=0)
        return dot(high, band[0]) + (dot(low, band[0]) + dot(high, band[1]))

    def edge_step(k, carry):
        wh, wl = [], []
        for i in range(per):
            at = pl.multiple_of((k * per + i) * SEG, SEG)
            for first in (0, BLOCK - 16):
                wh.append(xh[first : first + 16, pl.ds(at, 2 * SEG)])
                wl.append(xl[first : first + 16, pl.ds(at, 2 * SEG)])
        res = time_filter(wh, wl)
        for i in range(per):
            at = pl.multiple_of((k * per + i) * SEG, SEG)
            edge[0, :, pl.ds(at, SEG)] = res[32 * i : 32 * i + 2]
            edge[1, :, pl.ds(at, SEG)] = res[32 * i + 30 : 32 * i + 32]
        return carry

    lax.fori_loop(0, n_chunk, edge_step, 0)
    to_prev = pltpu.make_async_remote_copy(
        edge.at[0], rim.at[1], halo_s.at[1], halo_r.at[1],
        device_id=(prv, core), device_id_type=MESH_ID,
    )
    to_next = pltpu.make_async_remote_copy(
        edge.at[1], rim.at[0], halo_s.at[2], halo_r.at[2],
        device_id=(nxt, core), device_id_type=MESH_ID,
    )
    to_prev.start()
    to_next.start()

    def time_step(k, carry):
        wh, wl = [], []
        for i in range(per):
            at = pl.multiple_of((k * per + i) * SEG, SEG)
            wh.append(xh[:, pl.ds(at, 2 * SEG)])
            wl.append(xl[:, pl.ds(at, 2 * SEG)])
        res = time_filter(wh, wl)
        for i in range(per):
            at = pl.multiple_of((k * per + i) * SEG, SEG)
            tfb[8 : 8 + BLOCK, pl.ds(at, SEG)] = res[i * BLOCK : (i + 1) * BLOCK]
        return carry

    lax.fori_loop(0, n_chunk, time_step, 0)

    to_prev.wait()
    to_next.wait()
    tfb[6:8, :] = jnp.where(me > 0, rim[0], 0.0)
    tfb[8 + BLOCK : 10 + BLOCK, :] = jnp.where(me < n_chan - 1, rim[1], 0.0)

    def chunk_of(k):
        return pl.ds(k * per, per)

    def own_copy(k):
        return pltpu.make_async_copy(
            w.at[group, chunk_of(k)], r.at[2 + pos, core, chunk_of(k)], x_r.at[k, 0]
        )

    def x_copy(k, o):
        px, pc = peer(*offsets[o])
        return pltpu.make_async_remote_copy(
            w.at[px * CORES + pc, chunk_of(k)],
            r.at[2 + pos, core, chunk_of(k)],
            x_s.at[k, o],
            x_r.at[k, o],
            device_id=(line * GX + px, pc),
            device_id_type=MESH_ID,
        )

    def z_copy(k, way):
        if way == 0:
            src, dst, other = r.at[2:4, :, chunk_of(k)], r.at[6:8, :, chunk_of(k)], down
        else:
            src, dst, other = r.at[4:6, :, chunk_of(k)], r.at[0:2, :, chunk_of(k)], up
        return pltpu.make_async_remote_copy(
            src, dst, z_s.at[k, way], z_r.at[k, way],
            device_id=(other, core), device_id_type=MESH_ID,
        )

    def space_step(k, carry):
        for i in range(per):
            at = pl.multiple_of((k * per + i) * SEG, SEG)
            value = staps[0] * tfb[6 : 6 + BLOCK, pl.ds(at, SEG)]
            for tap in range(1, STAPS):
                value = value + staps[tap] * tfb[6 + tap : 6 + tap + BLOCK, pl.ds(at, SEG)]
            power = jnp.sum(value * value, axis=1, keepdims=True) * (1.0 / SEG)
            white = value * (1.0 / jnp.sqrt(power + 1e-05))
            w[:, k * per + i] = white.astype(BF16).reshape(GROUPS, QG, SEG)
        own_copy(k).start()
        for o in (4, 5, 2, 3, 6, 7, 1):
            x_copy(k, o).start()
        return carry

    lax.fori_loop(0, n_chunk, space_step, 0)

    c[...] = jnp.zeros_like(c)

    def receive(k):
        own_copy(k).wait()
        for o in range(1, GROUPS):
            x_copy(k, o).wait_recv()
        z_copy(k, 0).start()
        z_copy(k, 1).start()

    def correlate(k):
        z_copy(k, 0).wait_recv()
        z_copy(k, 1).wait_recv()

        def spectra(h, carry):
            rows = r[pl.ds(4 * h, 4), :, chunk_of(k)].reshape(4 * CORES * per * QG, SEG)
            xs[pl.ds(4 * h, 4)] = dot(rows, fwd[...]).reshape(4, CORES * per, QG, 2 * SEG)
            return carry

        lax.fori_loop(0, 2, spectra, 0)
        for qh in range(QG // 8):
            rows = slice(8 * qh, 8 * qh + 8)
            for kt in range(SEG // 128):
                re_at = slice(128 * kt, 128 * kt + 128)
                im_at = slice(SEG + 128 * kt, SEG + 128 * kt + 128)

                def step(s, acc):
                    re = [xs[b, s, rows, re_at] for b in range(WIN)]
                    im = [xs[b, s, rows, im_at] for b in range(WIN)]
                    new = []
                    for n, (i, j) in enumerate(OWN_PAIRS):
                        new.append(acc[2 * n] + (re[i] * re[j] + im[i] * im[j]))
                        new.append(acc[2 * n + 1] + (im[i] * re[j] - re[i] * im[j]))
                    return tuple(new)

                acc = []
                for n in range(N_OWN):
                    acc.append(c[n, rows, re_at])
                    acc.append(c[n, rows, im_at])
                acc = lax.fori_loop(0, CORES * per, step, tuple(acc))
                for n in range(N_OWN):
                    c[n, rows, re_at] = acc[2 * n]
                    c[n, rows, im_at] = acc[2 * n + 1]

    receive(0)

    def main_step(k, carry):
        receive(k)
        correlate(k - 1)
        return carry

    lax.fori_loop(1, n_chunk, main_step, 0)
    correlate(n_chunk - 1)

    high, low = halves(c[...].reshape(N_OWN * QG, 2 * SEG))
    lagged = dot(high, inv[0]) + (dot(low, inv[0]) + dot(high, inv[1]))
    pt[FROM_DN : FROM_DN + N_OWN] = lagged.astype(BF16).reshape(N_OWN, QG, SEG)
    to_down = pltpu.make_async_remote_copy(
        pt.at[FROM_DN : FROM_DN + FROM_UP],
        pt.at[FROM_DN + N_OWN : N_ALL],
        p_s.at[0], p_r.at[0], device_id=(down, core), device_id_type=MESH_ID,
    )
    to_up = pltpu.make_async_remote_copy(
        pt.at[FROM_DN + N_DOWN : FROM_DN + N_OWN],
        pt.at[0:FROM_DN],
        p_s.at[1], p_r.at[1], device_id=(up, core), device_id_type=MESH_ID,
    )
    to_down.start()
    to_up.start()

    for dx in range(1, GX):
        pair_copy(dx).wait()
    to_smem = pltpu.make_async_copy(pbv, pbs, pb_l)
    to_smem.start()
    to_smem.wait()
    to_down.wait()
    to_up.wait()

    def pick_step(n, carry):
        owner = n // SLOTS
        slot = n % SLOTS
        first = pbs[owner, slot, 0]
        second = pbs[owner, slot, 1]
        lowest = jnp.minimum(first, second) - (line - 1) * GX
        spot = jnp.clip(lowest * CUT + jnp.abs(first - second) - 1, 0, 12 * CUT - 1)
        f[n] = pt[lut[spot]]
        return carry

    lax.fori_loop(0, GX * SLOTS, pick_step, 0)

    half_slots = SLOTS // CORES

    def f_copy(o):
        px, pc = peer(*offsets[o])
        src = f.at[pl.ds(px * SLOTS + pc * half_slots, half_slots)]
        dst = g.at[:, group]
        if o == 0:
            return pltpu.make_async_copy(src, dst, f_r.at[0])
        return pltpu.make_async_remote_copy(
            src, dst, f_s.at[o], f_r.at[o],
            device_id=(line * GX + px, pc), device_id_type=MESH_ID,
        )

    for o in (4, 5, 2, 3, 6, 7, 1, 0):
        f_copy(o).start()
    f_copy(0).wait()
    for o in range(1, GROUPS):
        f_copy(o).wait()

    def out_step(i, carry):
        slot = core * half_slots + i
        back = (pairs[slot, 0] > pairs[slot, 1]).astype(jnp.int32)
        value = lax.dot_general(
            order[back],
            g[i].reshape(BLOCK, SEG),
            (((1,), (1,)), ((), ())),
            preferred_element_type=F32,
        )
        out[i] = jnp.where(slot < count[0], value[:LAGS], 0.0)
        return carry

    lax.fori_loop(0, half_slots, out_step, 0)

    def drain(k, carry):
        for o in range(1, GROUPS):
            x_copy(k, o).wait_send()
        z_copy(k, 0).wait_send()
        z_copy(k, 1).wait_send()
        return carry

    lax.fori_loop(0, n_chunk, drain, 0)


def local(n_chan, traces, channel_ok, time_taps, space_taps, pair_blocks, pair_count):
    samples = traces.shape[1]
    n_seg = samples // SEG
    n_chunk = min(4, n_seg)
    per = n_seg // n_chunk
    scale = 1.0 / math.sqrt(n_seg * CORES * SEG)
    smem = pl.BlockSpec(memory_space=pltpu.SMEM)
    vmem = pl.BlockSpec(memory_space=pltpu.VMEM)
    dma = pltpu.SemaphoreType.DMA
    return pl.pallas_call(
        functools.partial(kernel, n_chan),
        out_shape=jax.ShapeDtypeStruct((SLOTS // CORES, LAGS, BLOCK), F32),
        in_specs=[smem, smem, smem, smem, smem, vmem, vmem, vmem, vmem, vmem,
                  pl.BlockSpec(memory_space=pl.ANY)],
        out_specs=vmem,
        scratch_shapes=[
            pltpu.VMEM((BLOCK, samples + 2 * PAD), F32),
            pltpu.VMEM((BLOCK, samples + 2 * PAD), BF16),
            pltpu.VMEM((BLOCK, samples + 2 * PAD), BF16),
            pltpu.VMEM((2, 2 * SEG, SEG), BF16),
            pltpu.VMEM((2, 2, samples), F32),
            pltpu.VMEM((2, 2, samples), F32),
            pltpu.VMEM((BLOCK + 16, samples), F32),
            pltpu.VMEM((GROUPS, n_seg, QG, SEG), BF16),
            pltpu.VMEM((WIN, CORES, n_seg, QG, SEG), BF16),
            pltpu.VMEM((WIN, CORES * per, QG, 2 * SEG), F32),
            pltpu.VMEM((N_OWN, QG, 2 * SEG), F32),
            pltpu.VMEM((N_ALL, QG, SEG), BF16),
            pltpu.VMEM((GX * SLOTS, QG, SEG), BF16),
            pltpu.VMEM((SLOTS // CORES, GROUPS, QG, SEG), BF16),
            pltpu.VMEM((GX, SLOTS, 2), jnp.int32),
            pltpu.SMEM((GX, SLOTS, 2), jnp.int32),
            dma,
            dma((3,)),
            dma((3,)),
            dma((3,)),
            dma((3,)),
            dma,
            dma((n_chunk, GROUPS)),
            dma((n_chunk, GROUPS)),
            dma((n_chunk, 2)),
            dma((n_chunk, 2)),
            dma((2,)),
            dma((2,)),
            dma((GROUPS,)),
            dma((GROUPS,)),
        ],
        compiler_params=pltpu.CompilerParams(
            collective_id=0, has_side_effects=True, vmem_limit_bytes=48 * 1024 * 1024
        ),
    )(
        time_taps,
        space_taps,
        pair_blocks,
        pair_count,
        jnp.asarray(pair_positions()),
        channel_ok.reshape(1, BLOCK),
        pair_blocks,
        jnp.asarray(forward_np()),
        jnp.asarray(inverse_np(scale)),
        jnp.asarray(order_np()),
        traces,
    )


def solution(mesh):
    return jax.shard_map(
        functools.partial(local, mesh.shape["chan"]),
        mesh=mesh,
        in_specs=(P("chan", "tm"), P("chan"), P(), P(), P("chan", None), P("chan")),
        out_specs=P(("chan", "tm"), None, None),
        check_vma=False,
    )
```

time: 591 us -> 70.2 us (0.12)
  waiting for transfers between devices: 308 us -> 0 us
  other arithmetic: 153 us -> 0 us
  Pallas kernels: 0 us -> 60.3 us
  local copies, waits for them, and re-layouts: 54.1 us -> 9.03 us
  starting transfers between devices: 32.4 us -> 0 us
  loops' own time: 18.8 us -> 0 us
  between operations: 14.3 us -> 0.67 us
  matrix products: 8.49 us -> 0 us
    ppermute x12 -> x0, waiting for transfers between devices: 249 us -> none  [the longest x8 245 us: passed_along(): return lax.ppermute(block, axis, route)]
    pallas_call x0 -> x1, Pallas kernels: none -> 60.3 us  [local(): pl.pallas_call(functools.partial(kernel, n_chan), out_shape=jax.ShapeDtyp...]
    reduce_scatter x1 -> x0, waiting for transfers between devices: 59.4 us -> none  [local(): lagged = lax.psum_scatter(lagged_all, 'tm', scatter_dimension=0, tiled=True)]
    convert_element_type x18 -> x0, other arithmetic: 54.6 us -> none  [the longest x16 53.9 us: correlate(): left_spec = lax.dynamic_index_in_dim(window, first_block - owner_index +...]
    add x1 -> x0, other arithmetic: 43.2 us -> none  [local(): time_filtered + time_taps[tap_index] * padded[:, tap_index:tap_index + sa...]
    ppermute x12 -> x0, starting transfers between devices: 32.4 us -> none  [the longest x8 22.9 us: passed_along(): return lax.ppermute(block, axis, route)]
    dynamic_slice x48 -> x0, local copies, waits for them, and re-layouts: 27.8 us -> none  [local(): lax.map(correlate, (pair_blocks[:, 0], pair_blocks[:, 1], alive_flag))]
    reduce_sum x17 -> x0, other arithmetic: 23.6 us -> none  [the longest x16 21.7 us: correlate(): cross_re = jnp.sum(left_re * right_re + left_im * right_im, axis=1)]
  transfers between devices with their start and end apart: 13 -> 0, of which waited for: 7 -> 0; matrix products, arithmetic and copies ran while one was open for 3% -> 0% of each run, Pallas kernels for 0% -> 0%
where the time goes in v1:
time: 70.2 us; the launch traced here: 70 us
  Pallas kernels  60.3 us (86%)
  local copies, waits for them, and re-layouts  9.03 us (13%)
    pallas_call x1, Pallas kernels, local(): pl.pallas_call(functools.partial(kernel, n_chan), out_shape=jax.ShapeDtyp...  60.3 us
    unnamed x17, local copies, waits for them, and re-layouts  7.89 us

profile of v1, /device:TPU:1, one launch (start us, length us, event | category | flops | bytes accessed | tf_op | source)
XLA Modules:
  0.0 70.0 jit_solution(1099530158811707354)
XLA Ops:
  0.7 0.8 %copy.11.pairs.pairs_v = s32[16,2]{1,0:T(8,128)S(1)} copy(s32[16,2]{0,1:T(2,128)} %param.14) | data formatting | bytes 256 | tf_op args[4]
  1.4 0.0 copy-start
  1.4 1.6 %copy-done = f32[128,4096]{1,0:T(8,128)S(1)} copy-done((f32[128,4096]{1,0:T(8,128)S(1)}, f32[128,4096]{1,0:T(8,128)}, u32[]{:S(2)}) %copy-start) | copy-done | bytes 2097176
  3.0 0.0 copy-start.1
  3.0 1.0 %copy-done.1 = bf16[2,512,256]{2,1,0:T(8,128)(2,1)S(1)} copy-done((bf16[2,512,256]{2,1,0:T(8,128)(2,1)S(1)}, bf16[2,512,256]{2,1,0:T(8,128)(2,1)}, u32[]{:S(2)}) %copy-start.1) | copy-done | bytes 524312
  4.0 0.0 copy-start.2
  4.0 0.9 %copy-done.2 = bf16[256,512]{1,0:T(8,128)(2,1)S(1)} copy-done((bf16[256,512]{1,0:T(8,128)(2,1)S(1)}, bf16[256,512]{1,0:T(8,128)(2,1)}, u32[]{:S(2)}) %copy-start.2) | copy-done | bytes 262168
  5.0 0.0 copy-start.3
  5.0 0.9 %copy-done.3 = bf16[2,208,256]{2,1,0:T(8,128)(2,1)S(1)} copy-done((bf16[2,208,256]{2,1,0:T(8,128)(2,1)S(1)}, bf16[2,208,256]{2,1,0:T(8,128)(2,1)}, u32[]{:S(2)}) %copy-start.3) | copy-done | bytes 213016
  5.9 0.0 copy-start.4
  5.9 0.7 copy-done.4
  6.6 0.0 copy-start.5
  6.6 0.7 copy-done.5
  7.2 0.0 copy-start.6
  7.2 0.7 copy-done.6
  7.9 0.0 copy-start.7
  7.9 0.7 copy-done.7
  8.5 60.3 %shard_map.100 = f32[8,201,128]{2,1,0:T(8,128)S(1)} custom-call(f32[33]{0:T(128)S(1)} %copy-done.4, f32[5]{0:T(128)S(1)} %copy-done.5, s32[16,2]{1,0:T(8,128)S(1)} %copy.11.pairs.pairs_v, s32[1]{0:T(128)S(6)} %copy.14.count, s32[48]{0:T(128)S(1)} %copy-done.7, s32[1,128]{1,0:T(1,128)S(1)} %bitcast.1, s32[16,2]{1,0:T(8,128)S(1)} %copy.11.pairs.pairs_v, ...), custom_call_target="tpu_custom_call" | custom-call | tf_op jit(solution)/shard_map/pallas_call | solution.py:472
  68.8 1.1 %copy.13 = f32[8,201,128]{2,0,1:T(8,128)} copy(f32[8,201,128]{2,1,0:T(8,128)S(1)} %shard_map.100) | data formatting | bytes 1646592 | tf_op jit(solution)/shard_map/pallas_call | solution.py:472
Async XLA Ops:
  1.4 1.6 %copy-start = (f32[128,4096]{1,0:T(8,128)S(1)}, f32[128,4096]{1,0:T(8,128)}, u32[]{:S(2)}) copy-start(f32[128,4096]{1,0:T(8,128)} %traces.1) | copy-start | bytes 6291460
  3.0 1.0 %copy-start.1 = (bf16[2,512,256]{2,1,0:T(8,128)(2,1)S(1)}, bf16[2,512,256]{2,1,0:T(8,128)(2,1)}, u32[]{:S(2)}) copy-start(bf16[2,512,256]{2,1,0:T(8,128)(2,1)} %constant.10.clone.inv) | copy-start | bytes 1572868
  4.0 0.9 %copy-start.2 = (bf16[256,512]{1,0:T(8,128)(2,1)S(1)}, bf16[256,512]{1,0:T(8,128)(2,1)}, u32[]{:S(2)}) copy-start(bf16[256,512]{1,0:T(8,128)(2,1)} %constant.9.clone.fwd) | copy-start | bytes 786436
  5.0 0.9 %copy-start.3 = (bf16[2,208,256]{2,1,0:T(8,128)(2,1)S(1)}, bf16[2,208,256]{2,1,0:T(8,128)(2,1)}, u32[]{:S(2)}) copy-start(bf16[2,208,256]{2,1,0:T(8,128)(2,1)} %constant.11.clone.order) | copy-start | bytes 638980
  5.9 0.7 copy-start.4
  6.6 0.7 copy-start.5
  7.2 0.7 copy-start.6
  7.9 0.7 copy-start.7

commit v2 on v1

v2 whole, which is shorter than its diff:
```python
import functools
import math

import jax
import jax.numpy as jnp
import ml_dtypes
import numpy as np
from jax import lax
from jax.experimental import pallas as pl
from jax.experimental.pallas import tpu as pltpu
from jax.sharding import PartitionSpec as P

SEG = 256
MAXLAG = 100
TAPS = 33
STAPS = 5
CUT = 4
SLOTS = 16
NFFT = 510
LAGS = 201
LAGROWS = 208
BLOCK = 128
GX = 4
CORES = 2
GROUPS = GX * CORES
QG = BLOCK // GROUPS
WIN = 8
PAD = 128
HALF = (TAPS - 1) // 2
CHUNKS = 8

BF16 = jnp.bfloat16
F32 = jnp.float32
MESH_ID = pl.DeviceIdType.MESH

OWN_PAIRS = (
    [(i, j) for i in (0, 1) for j in range(2, 6) if j - i <= CUT]
    + [(i, j) for i in range(2, 6) for j in range(i + 1, 6)]
    + [(i, j) for i in (2, 3) for j in (6, 7) if j - i <= CUT]
)
N_DOWN = 7
N_IN = 6
N_UP = 3
N_OWN = len(OWN_PAIRS)
FROM_DN = N_IN + N_UP
FROM_UP = N_DOWN + N_IN
N_ALL = FROM_DN + N_OWN + FROM_UP


def pair_positions():
    table = np.zeros((12 * CUT,), np.int32)
    rel = [(i + 2, j + 2) for i, j in OWN_PAIRS]
    entries = (
        [(i - GX, j - GX) for i, j in rel[N_DOWN:]]
        + rel
        + [(i + GX, j + GX) for i, j in rel[: N_DOWN + N_IN]]
    )
    for spot, (low, high) in enumerate(entries):
        table[low * CUT + high - low - 1] = spot
    return table


def split_np(table):
    high = table.astype(ml_dtypes.bfloat16)
    low = (table - high.astype(np.float64)).astype(ml_dtypes.bfloat16)
    return np.stack([high, low])


def forward_np():
    phase = (np.arange(SEG)[:, None] * np.arange(SEG)[None, :] % NFFT) * (2.0 * np.pi / NFFT)
    return np.concatenate([np.cos(phase), -np.sin(phase)], axis=1).astype(ml_dtypes.bfloat16)


def inverse_np(scale):
    lag = np.arange(LAGS)[None, :] - MAXLAG
    bins = np.arange(SEG)[:, None]
    phase = (lag * bins % NFFT) * (2.0 * np.pi / NFFT)
    weight = np.where((bins == 0) | (bins == SEG - 1), 1.0, 2.0) / NFFT * scale
    table = np.zeros((2 * SEG, SEG), np.float64)
    table[:SEG, :LAGS] = weight * np.cos(phase)
    table[SEG:, :LAGS] = -weight * np.sin(phase)
    return split_np(table)


def order_np():
    table = np.zeros((2, LAGROWS, SEG), ml_dtypes.bfloat16)
    for lag in range(LAGS):
        table[0, lag, lag] = 1.0
        table[1, lag, LAGS - 1 - lag] = 1.0
    return table


def halves(value):
    high = value.astype(BF16)
    return high, (value - high.astype(F32)).astype(BF16)


def dot(a, b):
    return jnp.dot(a, b, preferred_element_type=F32)


def kernel(
    n_chan,
    taps_h,
    staps_h,
    pairs_h,
    count_h,
    lut_h,
    ok_h,
    fwd_h,
    inv_h,
    order_h,
    traces,
    out,
    taps,
    staps,
    pairs,
    count,
    lut,
    ok_row,
    fwd,
    inv,
    order,
    okn,
    xp,
    hx,
    xh,
    xl,
    hxh,
    hxl,
    band,
    tfb,
    w,
    r,
    xs,
    c,
    pt0,
    pt1,
    f,
    g,
    pbv,
    pbs,
    spots,
    in_sem,
    own_sem,
    halo_s,
    halo_r,
    pb_s,
    pb_r,
    pb_l,
    x_s,
    x_r,
    z_s,
    z_r,
    p_s,
    p_r,
    f_s,
    f_r,
):
    samples = traces.shape[1]
    n_seg = samples // SEG
    n_chunk = x_s.shape[0]
    per = n_seg // n_chunk
    lines = n_chan // GX
    me = lax.axis_index("chan")
    core = lax.axis_index("tm")
    line = me // GX
    pos = me % GX
    group = pos * CORES + core
    sibling = 1 - core
    nxt = (me + 1) % n_chan
    prv = (me + n_chan - 1) % n_chan
    up = ((line + 1) % lines) * GX + pos
    down = ((line + lines - 1) % lines) * GX + pos
    offsets = [(dx, dt) for dx in range(GX) for dt in range(CORES)]
    half_slots = SLOTS // CORES

    def peer(dx, dt):
        return (pos + dx) % GX, (core + dt) % CORES

    def remote(src, dst, send, recv, chan, tm):
        return pltpu.make_async_remote_copy(
            src, dst, send, recv, device_id=(chan, tm), device_id_type=MESH_ID
        )

    barrier = pltpu.get_barrier_semaphore()
    for dx, dt in offsets[1:]:
        px, pc = peer(dx, dt)
        pl.semaphore_signal(
            barrier, inc=1, device_id=(line * GX + px, pc), device_id_type=MESH_ID
        )
    for other in (up, down, nxt, prv):
        pl.semaphore_signal(barrier, inc=1, device_id=(other, core), device_id_type=MESH_ID)

    loads = [
        pltpu.make_async_copy(src, dst, in_sem.at[n])
        for n, (src, dst) in enumerate(
            [
                (taps_h, taps),
                (ok_h, ok_row),
                (traces, xp.at[:, pl.ds(PAD, samples)]),
                (staps_h, staps),
                (fwd_h, fwd),
                (pairs_h, pairs),
                (count_h, count),
                (lut_h, lut),
                (inv_h, inv),
                (order_h, order),
            ]
        )
    ]
    for load in loads:
        load.start()

    def at_of(j):
        return pl.multiple_of(jnp.where(core == 0, j, n_seg - 1 - j) * SEG, SEG)

    zero_at = pl.multiple_of(jnp.where(core == 0, 0, PAD + samples), PAD)
    pad_at = pl.multiple_of(jnp.where(core == 0, PAD + samples, 0), PAD)
    src_at = pl.multiple_of(jnp.where(core == 0, samples, PAD), PAD)
    xp[:, pl.ds(zero_at, PAD)] = jnp.zeros((BLOCK, PAD), F32)
    hx[:, pl.ds(zero_at, PAD)] = jnp.zeros((16, PAD), F32)

    loads[0].wait()
    band[...] = jnp.zeros_like(band)
    row = lax.broadcasted_iota(jnp.int32, (PAD, PAD), 0)
    col = lax.broadcasted_iota(jnp.int32, (PAD, PAD), 1)
    for diff in range(3):
        index = row - col + (PAD * diff - (PAD - HALF))
        tile = jnp.zeros((PAD, PAD), F32)
        for tap in range(TAPS):
            tile = jnp.where(index == tap, taps[tap], tile)
        high, low = halves(tile)
        for cb in range(2):
            rb = cb + diff
            band[0, rb * PAD : (rb + 1) * PAD, cb * PAD : (cb + 1) * PAD] = high
            band[1, rb * PAD : (rb + 1) * PAD, cb * PAD : (cb + 1) * PAD] = low
    loads[1].wait()
    okb = jnp.broadcast_to(ok_row[...], (BLOCK, BLOCK)).astype(F32)
    ok_col = jnp.sum(jnp.where(row == col, okb, 0.0), axis=1, keepdims=True)

    loads[2].wait()
    pl.semaphore_wait(barrier, len(offsets) - 1 + 4)

    to_next = remote(
        traces.at[BLOCK - 2 : BLOCK], hx.at[6:8, pl.ds(PAD, samples)],
        halo_s.at[1], halo_r.at[1], nxt, core,
    )
    to_prev = remote(
        traces.at[0:2], hx.at[8:10, pl.ds(PAD, samples)],
        halo_s.at[2], halo_r.at[2], prv, core,
    )
    ok_next = remote(ok_h, okn.at[0], halo_s.at[3], halo_r.at[3], nxt, core)
    ok_prev = remote(ok_h, okn.at[1], halo_s.at[4], halo_r.at[4], prv, core)
    halo = remote(
        xp.at[:, pl.ds(src_at, PAD)], xp.at[:, pl.ds(zero_at, PAD)],
        halo_s.at[0], halo_r.at[0], me, sibling,
    )
    corner_next = remote(
        xp.at[BLOCK - 2 : BLOCK, pl.ds(pad_at, PAD)], hx.at[6:8, pl.ds(pad_at, PAD)],
        halo_s.at[5], halo_r.at[5], nxt, core,
    )
    corner_prev = remote(
        xp.at[0:2, pl.ds(pad_at, PAD)], hx.at[8:10, pl.ds(pad_at, PAD)],
        halo_s.at[6], halo_r.at[6], prv, core,
    )

    def pair_copy(dx):
        return remote(
            pairs_h, pbv.at[pos], pb_s.at[dx - 1], pb_r.at[dx - 1],
            line * GX + (pos + dx) % GX, core,
        )

    own_pairs = pltpu.make_async_copy(pairs_h, pbv.at[pos], pb_l.at[0])
    to_smem = pltpu.make_async_copy(pbv, pbs, pb_l.at[1])

    for copy in (to_next, to_prev, ok_next, ok_prev, halo):
        copy.start()
    for dx in range(1, GX):
        pair_copy(dx).start()
    own_pairs.start()

    def mask_at(at):
        high, low = halves(xp[:, pl.ds(at, PAD)] * ok_col)
        xh[:, pl.ds(at, PAD)] = high
        xl[:, pl.ds(at, PAD)] = low

    def mask_step(i, carry):
        mask_at(pl.multiple_of((i + 1) * PAD, PAD))
        return carry

    lax.fori_loop(0, samples // PAD, mask_step, 0)
    mask_at(zero_at)

    def time_filter(windows_h, windows_l):
        high = jnp.concatenate(windows_h, axis=0)
        low = jnp.concatenate(windows_l, axis=0)
        return dot(high, band[0]) + (dot(low, band[0]) + dot(high, band[1]))

    def time_step(k):
        spot = [at_of(k * per + i) for i in range(per)]
        res = time_filter(
            [xh[:, pl.ds(at, 2 * SEG)] for at in spot],
            [xl[:, pl.ds(at, 2 * SEG)] for at in spot],
        )
        for i, at in enumerate(spot):
            tfb[8 : 8 + BLOCK, pl.ds(at, SEG)] = res[i * BLOCK : (i + 1) * BLOCK]

    def rim_step(steps):
        spot = [at_of(j) for j in steps]
        res = time_filter(
            [hxh[:, pl.ds(at, 2 * SEG)] for at in spot],
            [hxl[:, pl.ds(at, 2 * SEG)] for at in spot],
        )
        for i, at in enumerate(spot):
            tfb[0:8, pl.ds(at, SEG)] = res[16 * i : 16 * i + 8]
            tfb[8 + BLOCK : 16 + BLOCK, pl.ds(at, SEG)] = res[16 * i + 8 : 16 * i + 16]

    time_step(0)

    halo.wait()
    corner_next.start()
    corner_prev.start()
    mask_at(pad_at)

    for copy in (to_next, to_prev, ok_next, ok_prev):
        copy.wait()
    rim_row = lax.broadcasted_iota(jnp.int32, (16, BLOCK), 0)
    rim_col = lax.broadcasted_iota(jnp.int32, (16, BLOCK), 1)
    is_top = (rim_row >= 6) & (rim_row < 8) & (rim_col == rim_row + (BLOCK - 8)) & (me > 0)
    is_low = (rim_row >= 8) & (rim_row < 10) & (rim_col == rim_row - 8) & (me < n_chan - 1)
    ok_top = jnp.broadcast_to(okn[0], (16, BLOCK)).astype(F32)
    ok_low = jnp.broadcast_to(okn[1], (16, BLOCK)).astype(F32)
    ok_rim = jnp.sum(
        jnp.where(is_top, ok_top, jnp.where(is_low, ok_low, 0.0)), axis=1, keepdims=True
    )

    def rim_mask(at, width):
        rows = lax.broadcasted_iota(jnp.int32, (16, width), 0)
        high, low = halves(
            jnp.where((rows >= 6) & (rows < 10), hx[:, pl.ds(at, width)], 0.0) * ok_rim
        )
        hxh[:, pl.ds(at, width)] = high
        hxl[:, pl.ds(at, width)] = low

    def rim_mask_step(i, carry):
        rim_mask(pl.multiple_of(PAD + i * 2 * SEG, PAD), 2 * SEG)
        return carry

    lax.fori_loop(0, samples // (2 * SEG), rim_mask_step, 0)
    rim_mask(zero_at, PAD)
    rim_step(range(n_seg - 1))

    def chunk_of(k):
        return pl.ds(k * per, per)

    def own_copy(k):
        return pltpu.make_async_copy(
            w.at[group, chunk_of(k)], r.at[2 + pos, core, chunk_of(k)], own_sem.at[k]
        )

    def x_copy(k, o):
        px, pc = peer(*offsets[o])
        return remote(
            w.at[px * CORES + pc, chunk_of(k)], r.at[2 + pos, core, chunk_of(k)],
            x_s.at[k, o], x_r.at[k, o], line * GX + px, pc,
        )

    def z_copy(k, way):
        if way == 0:
            src, dst, other = r.at[2:4, :, chunk_of(k)], r.at[6:8, :, chunk_of(k)], down
        else:
            src, dst, other = r.at[4:6, :, chunk_of(k)], r.at[0:2, :, chunk_of(k)], up
        return remote(src, dst, z_s.at[k, way], z_r.at[k, way], other, core)

    def space_step(k):
        for i in range(per):
            at = at_of(k * per + i)
            value = staps[0] * tfb[6 : 6 + BLOCK, pl.ds(at, SEG)]
            for tap in range(1, STAPS):
                value = value + staps[tap] * tfb[6 + tap : 6 + tap + BLOCK, pl.ds(at, SEG)]
            power = jnp.sum(value * value, axis=1, keepdims=True) * (1.0 / SEG)
            white = value * (1.0 / jnp.sqrt(power + 1e-05))
            w[:, k * per + i] = white.astype(BF16).reshape(GROUPS, QG, SEG)
        for o in (4, 5, 2, 3, 6, 7, 1):
            x_copy(k, o).start()
        own_copy(k).start()

    def receive(k):
        own_copy(k).wait()
        for o in range(1, GROUPS):
            x_copy(k, o).wait_recv()
        z_copy(k, 0).start()
        z_copy(k, 1).start()

    def correlate(k):
        z_copy(k, 0).wait_recv()
        z_copy(k, 1).wait_recv()

        def spectra(h, carry):
            rows = r[pl.ds(4 * h, 4), :, chunk_of(k)].reshape(4 * CORES * per * QG, SEG)
            xs[pl.ds(4 * h, 4)] = dot(rows, fwd[...]).reshape(4, CORES * per, QG, 2 * SEG)
            return carry

        lax.fori_loop(0, 2, spectra, 0)
        for qh in range(QG // 8):
            rows = slice(8 * qh, 8 * qh + 8)
            for kt in range(SEG // 128):
                re_at = slice(128 * kt, 128 * kt + 128)
                im_at = slice(SEG + 128 * kt, SEG + 128 * kt + 128)

                def step(s, acc):
                    re = [xs[b, s, rows, re_at] for b in range(WIN)]
                    im = [xs[b, s, rows, im_at] for b in range(WIN)]
                    new = []
                    for n, (i, j) in enumerate(OWN_PAIRS):
                        new.append(acc[2 * n] + (re[i] * re[j] + im[i] * im[j]))
                        new.append(acc[2 * n + 1] + (im[i] * re[j] - re[i] * im[j]))
                    return tuple(new)

                acc = []
                for n in range(N_OWN):
                    acc.append(c[n, rows, re_at])
                    acc.append(c[n, rows, im_at])
                acc = lax.fori_loop(0, CORES * per, step, tuple(acc))
                for n in range(N_OWN):
                    c[n, rows, re_at] = acc[2 * n]
                    c[n, rows, im_at] = acc[2 * n + 1]

    def find_spots():
        for dx in range(1, GX):
            pair_copy(dx).wait()
        own_pairs.wait()
        for load in loads[3:]:
            if load is not loads[3] and load is not loads[4]:
                load.wait()
        to_smem.start()
        to_smem.wait()

        def spot_step(n, carry):
            owner = n // SLOTS
            slot = n % SLOTS
            first = pbs[owner, 0, slot]
            second = pbs[owner, 1, slot]
            lowest = jnp.minimum(first, second) - (line - 1) * GX
            index = jnp.clip(lowest * CUT + jnp.abs(first - second) - 1, 0, 12 * CUT - 1)
            spots[n] = lut[index]
            return carry

        lax.fori_loop(0, GX * SLOTS, spot_step, 0)

    c[...] = jnp.zeros_like(c)
    loads[3].wait()
    loads[4].wait()

    def tick(i, carry):
        @pl.when(i < n_chunk)
        def _():
            space_step(i)

        @pl.when((i >= 2) & (i < n_chunk + 2))
        def _():
            receive(i - 2)

        @pl.when(i + 1 < n_chunk)
        def _():
            time_step(i + 1)

        @pl.when(i == n_chunk - 2)
        def _():
            corner_next.wait()
            corner_prev.wait()
            rim_mask(pad_at, PAD)
            rim_step([n_seg - 1])

        @pl.when(i == 3)
        def _():
            find_spots()

        @pl.when(i >= 4)
        def _():
            correlate(i - 4)

        return carry

    lax.fori_loop(0, n_chunk + 4, tick, 0)

    pt = (pt0, pt1)

    def to_down(h):
        return remote(
            pt[h].at[FROM_DN : FROM_DN + FROM_UP], pt[h].at[FROM_DN + N_OWN : N_ALL],
            p_s.at[h, 0], p_r.at[h, 0], down, core,
        )

    def to_up(h):
        return remote(
            pt[h].at[FROM_DN + N_DOWN : FROM_DN + N_OWN], pt[h].at[0:FROM_DN],
            p_s.at[h, 1], p_r.at[h, 1], up, core,
        )

    for h in range(2):
        high, low = halves(c[:, 8 * h : 8 * h + 8].reshape(N_OWN * 8, 2 * SEG))
        lagged = dot(high, inv[0]) + (dot(low, inv[0]) + dot(high, inv[1]))
        pt[h][FROM_DN : FROM_DN + N_OWN] = lagged.astype(BF16).reshape(N_OWN, 8, SEG)
        to_down(h).start()
        to_up(h).start()

    def f_copy(h, o):
        px, pc = peer(*offsets[o])
        src = f.at[h, pl.ds(px * SLOTS + pc * half_slots, half_slots)]
        dst = g.at[:, group, h]
        if o == 0:
            return pltpu.make_async_copy(src, dst, f_r.at[h, 0])
        return remote(src, dst, f_s.at[h, o], f_r.at[h, o], line * GX + px, pc)

    for h in range(2):
        to_down(h).wait()
        to_up(h).wait()

        def pick_step(n, carry):
            for i in range(8):
                f[h, n * 8 + i] = pt[h][spots[n * 8 + i]]
            return carry

        lax.fori_loop(0, GX * SLOTS // 8, pick_step, 0)
        for o in (4, 5, 2, 3, 6, 7, 1, 0):
            f_copy(h, o).start()

    def drain(k, carry):
        for o in range(1, GROUPS):
            x_copy(k, o).wait_send()
        z_copy(k, 0).wait_send()
        z_copy(k, 1).wait_send()
        return carry

    lax.fori_loop(0, n_chunk, drain, 0)
    for h in range(2):
        for o in range(GROUPS):
            f_copy(h, o).wait()

    for i in range(half_slots):
        slot = core * half_slots + i
        back = (pairs[0, slot] > pairs[1, slot]).astype(jnp.int32)
        value = lax.dot_general(
            order[back],
            g[i].reshape(BLOCK, SEG),
            (((1,), (1,)), ((), ())),
            preferred_element_type=F32,
        )
        out[:, i, :] = jnp.where(slot < count[0], value[:LAGS], 0.0)


def local(n_chan, traces, channel_ok, time_taps, space_taps, pair_blocks, pair_count):
    samples = traces.shape[1]
    n_seg = samples // SEG
    n_chunk = CHUNKS
    per = n_seg // n_chunk
    scale = 1.0 / math.sqrt(n_seg * CORES * SEG)
    hbm = pl.BlockSpec(memory_space=pltpu.HBM)
    dma = pltpu.SemaphoreType.DMA
    wide = samples + 2 * PAD
    half_slots = SLOTS // CORES
    res = pl.pallas_call(
        functools.partial(kernel, n_chan),
        out_shape=jax.ShapeDtypeStruct((LAGS, half_slots, BLOCK), F32),
        in_specs=[hbm] * 10,
        out_specs=pl.BlockSpec(memory_space=pltpu.VMEM),
        scratch_shapes=[
            pltpu.SMEM((TAPS,), F32),
            pltpu.SMEM((STAPS,), F32),
            pltpu.SMEM((2, SLOTS), jnp.int32),
            pltpu.SMEM((1,), jnp.int32),
            pltpu.SMEM((12 * CUT,), jnp.int32),
            pltpu.VMEM((1, BLOCK), jnp.int32),
            pltpu.VMEM((SEG, 2 * SEG), BF16),
            pltpu.VMEM((2, 2 * SEG, SEG), BF16),
            pltpu.VMEM((2, LAGROWS, SEG), BF16),
            pltpu.VMEM((2, 1, BLOCK), jnp.int32),
            pltpu.VMEM((BLOCK, wide), F32),
            pltpu.VMEM((16, wide), F32),
            pltpu.VMEM((BLOCK, wide), BF16),
            pltpu.VMEM((BLOCK, wide), BF16),
            pltpu.VMEM((16, wide), BF16),
            pltpu.VMEM((16, wide), BF16),
            pltpu.VMEM((2, 2 * SEG, SEG), BF16),
            pltpu.VMEM((BLOCK + 16, samples), F32),
            pltpu.VMEM((GROUPS, n_seg, QG, SEG), BF16),
            pltpu.VMEM((WIN, CORES, n_seg, QG, SEG), BF16),
            pltpu.VMEM((WIN, CORES * per, QG, 2 * SEG), F32),
            pltpu.VMEM((N_OWN, QG, 2 * SEG), F32),
            pltpu.VMEM((N_ALL, 8, SEG), BF16),
            pltpu.VMEM((N_ALL, 8, SEG), BF16),
            pltpu.VMEM((2, GX * SLOTS, 8, SEG), BF16),
            pltpu.VMEM((half_slots, GROUPS, 2, 8, SEG), BF16),
            pltpu.VMEM((GX, 2, SLOTS), jnp.int32),
            pltpu.SMEM((GX, 2, SLOTS), jnp.int32),
            pltpu.SMEM((GX * SLOTS,), jnp.int32),
            dma((10,)),
            dma((n_chunk,)),
            dma((7,)),
            dma((7,)),
            dma((3,)),
            dma((3,)),
            dma((2,)),
            dma((n_chunk, GROUPS)),
            dma((n_chunk, GROUPS)),
            dma((n_chunk, 2)),
            dma((n_chunk, 2)),
            dma((2, 2)),
            dma((2, 2)),
            dma((2, GROUPS)),
            dma((2, GROUPS)),
        ],
        compiler_params=pltpu.CompilerParams(
            collective_id=0, has_side_effects=True, vmem_limit_bytes=67043328
        ),
    )(
        time_taps,
        space_taps,
        jnp.transpose(pair_blocks),
        pair_count,
        jnp.asarray(pair_positions()),
        channel_ok.reshape(1, BLOCK),
        jnp.asarray(forward_np()),
        jnp.asarray(inverse_np(scale)),
        jnp.asarray(order_np()),
        traces,
    )
    return jnp.transpose(res, (1, 0, 2))


def solution(mesh):
    return jax.shard_map(
        functools.partial(local, mesh.shape["chan"]),
        mesh=mesh,
        in_specs=(P("chan", "tm"), P("chan"), P(), P(), P("chan", None), P("chan")),
        out_specs=P(("chan", "tm"), None, None),
        check_vma=False,
    )
```

time: 70.2 us -> 60.3 us (0.86)
  local copies, waits for them, and re-layouts: 9.03 us -> 2.09 us
  Pallas kernels: 60.3 us -> 57.4 us
    unnamed x17 -> x1, local copies, waits for them, and re-layouts: 7.89 us -> 2.09 us
    pallas_call x1, Pallas kernels: 60.3 us -> 57.4 us  [local(): pl.pallas_call(functools.partial(kernel, n_chan), out_shape=jax.ShapeDtyp...]
    pallas_call x1 -> x0, local copies, waits for them, and re-layouts: 1.15 us -> none  [local(): pl.pallas_call(functools.partial(kernel, n_chan), out_shape=jax.ShapeDtyp...]
where the time goes in v2:
time: 60.3 us; the launch traced here: 60.2 us
  Pallas kernels  57.4 us (95%)
  local copies, waits for them, and re-layouts  2.09 us (3%)
  between operations  0.66 us (1%)
    pallas_call x1, Pallas kernels, local(): pl.pallas_call(functools.partial(kernel, n_chan), out_shape=jax.ShapeDtyp...  57.4 us
    unnamed x1, local copies, waits for them, and re-layouts  2.09 us

profile of v2, /device:TPU:1, one launch (start us, length us, event | category | flops | bytes accessed | tf_op | source)
XLA Modules:
  0.0 60.2 jit_solution(5819020581382902876)
XLA Ops:
  0.7 57.4 %shard_map.100 = f32[201,8,128]{2,1,0:T(8,128)} custom-call(f32[33]{0:T(128)} %taps_h.1, f32[5]{0:T(128)} %staps_h.1, s32[2,16]{1,0:T(2,128)} %bitcast.4, s32[1]{0:T(128)S(6)} %copy.12.count_h, s32[48]{0:T(128)} %constant.8.clone.lut_h, s32[1,128]{1,0:T(1,128)} %bitcast.5, bf16[256,512]{1,0:T(8,128)(2,1)} %constant.9.clone.fwd_h, ...), custom_call_target="tpu_custom_call" | custom-call | tf_op jit(solution)/shard_map/pallas_call | solution.py:564
  58.1 2.1 %copy.13 = f32[8,201,128]{2,0,1:T(8,128)} copy(f32[8,201,128]{2,0,1:T(8,128)} %bitcast.3) | data formatting | bytes 1646592
